TPU v7x, 32 devices: a whole 2x2x4 slice. The times are simulated.
32 devices in a mesh: groups: 2 (over x), ctx: 16 (over z, y, core).
Axes of the slice: x: 2, y: 2, z: 4, core: 2. Of those that a mesh axis runs over, the one named last changes fastest.
Arguments:
- queries: bfloat16 [4096, 2048], P(('groups', 'ctx')), parts along dimension 0, may hold values from -6 to 6
- keys: bfloat16 [4096, 2048], P(('groups', 'ctx')), parts along dimension 0, may hold values from -6 to 6
- values: bfloat16 [4096, 2048], P(('groups', 'ctx')), parts along dimension 0, may hold values from -6 to 6
- out_grad: bfloat16 [4096, 2048], P(('groups', 'ctx')), parts along dimension 0, may hold values from -6 to 6
- conv_weight: float32 [8, 16], replicated, may hold values from -2 to 2
Outputs:
- dq: bfloat16 [4096, 2048], P(('groups', 'ctx')), parts along dimension 0
- dk: bfloat16 [4096, 2048], P(('groups', 'ctx')), parts along dimension 0
- dv: bfloat16 [4096, 2048], P(('groups', 'ctx')), parts along dimension 0
- dconv: float32 [16, 16], P('groups'), parts along dimension 0
There are 2 independent parts, one for each index of `groups`. A program takes and returns all parts, laid end to end along the dimension named above; an argument that names none is the same for every part. Nothing has to cross between parts.
All inputs are finite; a program needn't handle non-finite values.
Results may differ from a plain program's by a relative error of at most 0.024.
Values may be sent and summed in bfloat16 or wider, within the bound.
A program may use at most 128 MiB of HBM per device.

v0:
```python
import jax
import jax.numpy as jnp
from jax import lax
from jax.sharding import PartitionSpec as P


def compress(rows, conv_weight):
    count = rows.shape[0]
    stride, heads = conv_weight.shape
    shaped = rows.reshape(count // stride, stride, heads, -1).astype(jnp.float32)
    merged = jnp.einsum("cshd,sh->chd", shaped, conv_weight).astype(jnp.bfloat16)
    return merged.reshape(count // stride, -1)


def local(queries, keys, values, out_grad, conv_weight):
    count, width = queries.shape
    stride, heads = conv_weight.shape
    head_dim = width // heads
    rows_mem = count // stride
    scale = head_dim ** (-0.5)
    shard_id = lax.axis_index("ctx")
    total_mem = rows_mem * lax.axis_size("ctx")
    q3 = queries.reshape(count, heads, head_dim)
    k3 = keys.reshape(count, heads, head_dim)
    v3 = values.reshape(count, heads, head_dim)
    g3 = out_grad.reshape(count, heads, head_dim)
    mem_keys = compress(keys, conv_weight)
    mem_vals = compress(values, conv_weight)
    causal = jnp.arange(count)[:, None] >= jnp.arange(count)[None, :]
    local_scores = jnp.einsum("shd,thd->hst", q3, k3, preferred_element_type=jnp.float32) * scale
    local_scores = jnp.where(causal[None], local_scores, -1e30)
    high0 = local_scores.max(-1)
    local_prob = jnp.where(causal[None], jnp.exp(local_scores - high0[..., None]), 0.0)
    total0 = local_prob.sum(-1)
    accum0 = jnp.einsum("hst,thd->hsd", local_prob, v3.astype(jnp.float32))

    def score_block(block_keys):
        rows = block_keys.shape[0]
        keys_block = block_keys.reshape(rows, heads, head_dim)
        valid = jnp.arange(rows, dtype=jnp.int32) // rows_mem < shard_id
        scores = (
            jnp.einsum("shd,nhd->hsn", q3, keys_block, preferred_element_type=jnp.float32) * scale
        )
        return (valid, scores)

    all_keys, all_vals = (
        lax.all_gather(mem_keys, "ctx", axis=0, tiled=True),
        lax.all_gather(mem_vals, "ctx", axis=0, tiled=True),
    )
    high = high0
    total = total0
    accum = accum0
    rows = all_keys.shape[0]
    valid, scores = score_block(all_keys)
    scores = jnp.where(valid[None, None, :], scores, -1e30)
    new_high = jnp.maximum(high, scores.max(-1))
    prob = jnp.where(valid[None, None, :], jnp.exp(scores - new_high[..., None]), 0.0)
    factor = jnp.exp(high - new_high)
    vals_block = all_vals.reshape(rows, heads, head_dim)
    total = total * factor + prob.sum(-1)
    accum = accum * factor[..., None] + jnp.einsum(
        "hsn,nhd->hsd", prob, vals_block, preferred_element_type=jnp.float32
    )
    stats = (new_high, total, accum)
    high, total, accum = stats
    lse = high + jnp.log(total)
    output = accum / total[..., None]
    dsum = jnp.einsum("hsd,shd->hs", output, g3.astype(jnp.float32))
    valid_all, scores_all = score_block(all_keys)
    mem_prob = jnp.where(valid_all[None, None, :], jnp.exp(scores_all - lse[..., None]), 0.0)
    keys_all = all_keys.reshape(total_mem, heads, head_dim)
    vals_all = all_vals.reshape(total_mem, heads, head_dim)
    mem_dprob = jnp.einsum("shd,nhd->hsn", g3, vals_all, preferred_element_type=jnp.float32)
    mem_ds = (mem_prob * (mem_dprob - dsum[..., None])).astype(jnp.bfloat16)
    mem_pb = mem_prob.astype(jnp.bfloat16)
    dq_mem = jnp.einsum("hsn,nhd->shd", mem_ds, keys_all, preferred_element_type=jnp.float32)
    dk_part = jnp.einsum("hsn,shd->nhd", mem_ds, q3, preferred_element_type=jnp.float32) * scale
    dv_part = jnp.einsum("hsn,shd->nhd", mem_pb, g3, preferred_element_type=jnp.float32)
    summed = lax.psum_scatter(
        jnp.concatenate(
            (dk_part.reshape(total_mem, width), dv_part.reshape(total_mem, width)), axis=1
        ),
        "ctx",
        scatter_dimension=0,
        tiled=True,
    )
    dmem_k = summed[:, :width].reshape(rows_mem, heads, head_dim)
    dmem_v = summed[:, width:].reshape(rows_mem, heads, head_dim)
    local_p = jnp.where(causal[None], jnp.exp(local_scores - lse[..., None]), 0.0)
    local_dp = jnp.einsum("shd,thd->hst", g3, v3, preferred_element_type=jnp.float32)
    local_ds = (local_p * (local_dp - dsum[..., None])).astype(jnp.bfloat16)
    dq_all = (
        dq_mem + jnp.einsum("hst,thd->shd", local_ds, k3, preferred_element_type=jnp.float32)
    ) * scale
    dk_local = jnp.einsum("hst,shd->thd", local_ds, q3, preferred_element_type=jnp.float32) * scale
    dv_local = jnp.einsum(
        "hst,shd->thd", local_p.astype(jnp.bfloat16), g3, preferred_element_type=jnp.float32
    )
    spread_k = jnp.einsum("chd,sh->cshd", dmem_k, conv_weight).reshape(count, heads, head_dim)
    spread_v = jnp.einsum("chd,sh->cshd", dmem_v, conv_weight).reshape(count, heads, head_dim)
    dq = dq_all.reshape(count, width).astype(jnp.bfloat16)
    dk = (dk_local + spread_k).reshape(count, width).astype(jnp.bfloat16)
    dv = (dv_local + spread_v).reshape(count, width).astype(jnp.bfloat16)
    key_rows = keys.reshape(rows_mem, stride, heads, head_dim).astype(jnp.float32)
    val_rows = values.reshape(rows_mem, stride, heads, head_dim).astype(jnp.float32)
    partial_conv = jnp.einsum("chd,cshd->sh", dmem_k, key_rows) + jnp.einsum(
        "chd,cshd->sh", dmem_v, val_rows
    )
    dconv = lax.psum(partial_conv, "ctx")
    return (dq, dk, dv, dconv)


def solution(mesh):
    return jax.shard_map(
        local,
        mesh=mesh,
        in_specs=(
            P(("groups", "ctx"), None),
            P(("groups", "ctx"), None),
            P(("groups", "ctx"), None),
            P(("groups", "ctx"), None),
            P(),
        ),
        out_specs=(
            P(("groups", "ctx"), None),
            P(("groups", "ctx"), None),
            P(("groups", "ctx"), None),
            P("groups", None),
        ),
        check_vma=False,
    )
```

profile of v0, /device:TPU:0, one launch (start us, length us, event | category | flops | bytes accessed | tf_op | source)
XLA Modules:
  0.0 238.7 jit_solution(13422166051931242764)
XLA Ops:
  7.2 0.8 copy.90
  8.1 1.4 fusion.38
  10.2 1.3 fusion.36
  13.0 1.2 copy.80
  14.7 1.0 copy-done
  15.9 35.5 %all-gather.3.cloned.1.call-done = bf16[256,2048]{1,0:T(8,128)(2,1)} async-done(((bf16[16,2048]{1,0:T(8,128)(2,1)}), bf16[256,2048]{1,0:T(8,128)(2,1)}) %all-gather.3.cloned.1.call-update) | async-done | bytes 1048592 | tf_op jit(solution)/shard_map/all_gather | solution.py:47
  51.4 2.3 copy.58
  53.6 1.8 bitcast_reduce_fusion
  56.1 34.3 %all-gather.5.cloned.1.call-done = bf16[256,2048]{1,0:T(8,128)(2,1)} async-done(((bf16[16,2048]{1,0:T(8,128)(2,1)}), bf16[256,2048]{1,0:T(8,128)(2,1)}) %all-gather.5.cloned.1.call-update) | async-done | bytes 1048592 | tf_op jit(solution)/shard_map/all_gather | solution.py:48
  90.4 2.3 copy.63
  92.7 2.2 fusion.3
  94.9 0.8 fusion.13
  96.5 3.1 %fusion.19 = f32[16,256,128]{1,2,0:T(8,128)} fusion(bf16[128,16,128]{0,2,1:T(8,128)(2,1)} %copy.80, f32[16,256,128]{2,1,0:T(8,128)S(1)} %get-tuple-element.26, f32[16,128]{1,0:T(8,128)S(1)} %get-tuple-element.16, pred[256]{0:T(512)(128)(4,1)S(1)} %fusion.48), kind=kOutput, calls=%fused_computation.31 | convolution fusion | flops 136314880 | bytes 4727040 | tf_op jit(solution)/shard_map/hsn,shd->nhd/dot_general | solution.py:78
  99.6 0.9 multiply_convert_fusion
  100.5 1.0 copy-done.10
  101.9 1.8 copy.79
  103.7 4.5 %pad_maximum_fusion = f32[256,4096]{0,1:T(8,128)} fusion(f32[256,2048]{0,1:T(8,128)} %bitcast.140, f32[256,2048]{0,1:T(8,128)} %bitcast.141), kind=kLoop, calls=%fused_computation | loop fusion | flops 1048576 | bytes 8388608 | tf_op jit(solution)/shard_map/concatenate | solution.py:80
  108.2 5.6 %copy.125 = f32[256,4096]{1,0:T(8,128)} copy(f32[256,4096]{0,1:T(8,128)} %pad_maximum_fusion) | data formatting | bytes 8388608
  113.8 1.2 copy-done.2
  115.0 1.6 fusion.17
  117.2 0.8 copy-done.9
  118.3 1.0 copy.87
  119.3 66.5 %reduce-scatter.4.cloned.1.call-done = f32[16,4096]{1,0:T(8,128)} async-done(((f32[256,4096]{1,0:T(8,128)}), f32[16,4096]{1,0:T(8,128)}) %reduce-scatter.4.cloned.1.call-update) | async-done | bytes 262160
  185.8 1.0 fusion.56
  187.8 1.3 multiply_reduce_fusion
  191.6 30.1 %psum.7 = f32[8,16]{1,0:T(8,128)} all-reduce(f32[8,16]{1,0:T(8,128)S(1)} %add_bitcast_fusion), channel_id=1, replica_groups=mesh['groups'=2,'ctx'=16] {'ctx'}, use_global_device_ids=true, to_apply=%region_5.6 | all-reduce | flops 128 | bytes 1024 | tf_op jit(solution)/shard_map/psum | solution.py:109
  221.7 2.4 broadcast_multiply_fusion
  224.1 1.6 copy.86
  225.7 1.3 fusion.18
  227.0 2.1 copy.89
  229.1 1.6 copy.82
  231.2 1.0 copy.88
  (72 shorter events, 9.5 us)
Async XLA Ops:
  7.2 5.2 %copy-start.4 = (bf16[128,2048]{1,0:T(8,128)(2,1)S(1)}, bf16[128,2048]{1,0:T(8,128)(2,1)}, u32[]{:S(2)}) copy-start(bf16[128,2048]{1,0:T(8,128)(2,1)} %param.6) | copy-start | bytes 1572868
  7.2 5.5 %copy-start.16 = (bf16[128,2048]{1,0:T(8,128)(2,1)S(1)}, bf16[128,2048]{1,0:T(8,128)(2,1)}, u32[]{:S(2)}) copy-start(bf16[128,2048]{1,0:T(8,128)(2,1)} %param.5) | copy-start | bytes 1572868
  7.2 44.2 %all-gather.3.cloned.1.call-start = ((), (), s32[]{:S(2)}) async-start(), calls=%async_computation.1 | async-start | bytes 1114112 | tf_op jit(solution)/shard_map/all_gather | solution.py:47
  8.1 4.8 %copy-start.17 = (bf16[128,2048]{1,0:T(8,128)(2,1)S(1)}, bf16[128,2048]{1,0:T(8,128)(2,1)}, u32[]{:S(2)}) copy-start(bf16[128,2048]{1,0:T(8,128)(2,1)} %param.8) | copy-start | bytes 1572868
  10.2 80.2 %all-gather.5.cloned.1.call-start = ((), (), s32[]{:S(2)}) async-start(), calls=%async_computation.2 | async-start | bytes 1114112 | tf_op jit(solution)/shard_map/all_gather | solution.py:48
  12.3 173.5 %reduce-scatter.4.cloned.1.call-start = ((), (), s32[]{:S(2)}) async-start(), calls=%async_computation.3 | async-start | bytes 4456448
  12.6 2.1 copy-start.8
  14.7 1.0 copy-start
  92.7 2.2 copy-start.1
  92.7 2.2 copy-start.14
  94.9 19.0 %copy-start.18 = (f32[16,128]{1,0:T(8,128)}, f32[16,128]{1,0:T(8,128)S(1)}, u32[]{:S(2)}) copy-start(f32[16,128]{1,0:T(8,128)S(1)} %get-tuple-element.16) | copy-start | bytes 24580
  96.5 3.1 %copy-start.6 = (bf16[128,16,128]{0,2,1:T(8,128)(2,1)S(1)}, bf16[128,16,128]{0,2,1:T(8,128)(2,1)}, u32[]{:S(2)}) copy-start(bf16[128,16,128]{0,2,1:T(8,128)(2,1)} %copy.80) | copy-start | bytes 1572868
  96.5 3.1 %copy-start.15 = (bf16[256,2048]{0,1:T(8,128)(2,1)S(1)}, bf16[256,2048]{0,1:T(8,128)(2,1)}, u32[]{:S(2)}) copy-start(bf16[256,2048]{0,1:T(8,128)(2,1)} %copy.63) | copy-start | bytes 3145732
  100.5 1.0 copy-start.10
  113.8 1.2 copy-start.2
  115.0 1.6 copy-start.3
  115.0 1.7 copy-start.11
  116.7 1.5 copy-start.12
  116.7 1.2 copy-start.9
  187.7 2.9 %copy-start.5 = (bf16[128,2048]{1,0:T(8,128)(2,1)S(1)}, bf16[128,2048]{1,0:T(8,128)(2,1)}, u32[]{:S(2)}) copy-start(bf16[128,2048]{1,0:T(8,128)(2,1)} %param.6) | copy-start | bytes 1572868
  221.7 4.0 %copy-start.7 = (bf16[128,16,128]{0,2,1:T(8,128)(2,1)S(1)}, bf16[128,16,128]{0,2,1:T(8,128)(2,1)}, u32[]{:S(2)}) copy-start(bf16[128,16,128]{0,2,1:T(8,128)(2,1)} %copy.80) | copy-start | bytes 1572868
  221.7 4.0 %copy-start.19 = (f32[16,128]{1,0:T(8,128)S(1)}, f32[16,128]{1,0:T(8,128)}, u32[]{:S(2)}) copy-start(f32[16,128]{1,0:T(8,128)} %copy-done.18) | copy-start | bytes 24580
  227.0 3.7 %copy-start.13 = (bf16[16,128,128]{1,2,0:T(8,128)(2,1)S(1)}, bf16[16,128,128]{1,2,0:T(8,128)(2,1)}, u32[]{:S(2)}) copy-start(bf16[16,128,128]{1,2,0:T(8,128)(2,1)} %copy-done.12) | copy-start | bytes 1572868
Sparse Core Ops, SparseCore 0:
  10.7 40.5 all-gather.2
  53.5 36.8 all-gather.4
  114.0 71.7 reduce-scatter.3
where the time goes:
time: 239 us
  waiting for transfers between devices  136 us (57%)
  local copies, waits for them, and re-layouts  31.1 us (13%)
  blocking collectives  30.1 us (13%)
  matrix products  16.4 us (7%)
  between operations  14.1 us (6%)
  other arithmetic  10.6 us (4%)
    unnamed x4, waiting for transfers between devices  66.5 us
    all_gather x1, waiting for transfers between devices, local(): lax.all_gather(mem_keys, 'ctx', axis=0, tiled=True)  35.5 us
    all_gather x1, waiting for transfers between devices, local(): lax.all_gather(mem_vals, 'ctx', axis=0, tiled=True)  34.3 us
    psum x1, blocking collectives, local(): dconv = lax.psum(partial_conv, 'ctx')  30.1 us
    unnamed x52, local copies, waits for them, and re-layouts  17.3 us
  transfers between devices with their start and end apart: 3, of which 3 were waited for; matrix products, arithmetic and copies ran while one was open for 5% of the time, Pallas kernels for 0%

commit v1 on v0

--- a/solution.py
+++ b/solution.py
@@ -106,7 +106,7 @@
     partial_conv = jnp.einsum("chd,cshd->sh", dmem_k, key_rows) + jnp.einsum(
         "chd,cshd->sh", dmem_v, val_rows
     )
-    dconv = lax.psum(partial_conv, "ctx")
+    dconv = jnp.sum(lax.all_gather(partial_conv, "ctx"), axis=0)
     return (dq, dk, dv, dconv)
 
 

time: 239 us -> 229 us (0.958)
  blocking collectives: 30.1 us -> 19.2 us
    psum x1 -> x0, blocking collectives: 30.1 us -> none  [local(): dconv = lax.psum(partial_conv, 'ctx')]
    all_gather x0 -> x1, blocking collectives: none -> 19.2 us  [local(): dconv = jnp.sum(lax.all_gather(partial_conv, 'ctx'), axis=0)]
where the time goes in v1:
time: 229 us; the launch traced here: 228 us
  waiting for transfers between devices  136 us (59%)
  local copies, waits for them, and re-layouts  31.1 us (14%)
  blocking collectives  19.2 us (8%)
  matrix products  16.4 us (7%)
  between operations  14.1 us (6%)
  other arithmetic  11.2 us (5%)
    unnamed x4, waiting for transfers between devices  66.5 us
    all_gather x1, waiting for transfers between devices, local(): lax.all_gather(mem_keys, 'ctx', axis=0, tiled=True)  35.5 us
    all_gather x1, waiting for transfers between devices, local(): lax.all_gather(mem_vals, 'ctx', axis=0, tiled=True)  34.3 us
    all_gather x1, blocking collectives, local(): dconv = jnp.sum(lax.all_gather(partial_conv, 'ctx'), axis=0)  19.2 us
    unnamed x52, local copies, waits for them, and re-layouts  17.3 us
  transfers between devices with their start and end apart: 3, of which 3 were waited for; matrix products, arithmetic and copies ran while one was open for 5% of the time, Pallas kernels for 0%

profile of v1, /device:TPU:0, one launch (start us, length us, event | category | flops | bytes accessed | tf_op | source)
XLA Modules:
  0.0 228.5 jit_solution(6120559144007948147)
XLA Ops:
  7.2 0.8 copy.90
  8.1 1.4 fusion.38
  10.2 1.3 fusion.36
  13.0 1.2 copy.80
  14.7 1.0 copy-done
  15.9 35.5 %all-gather.4.cloned.1.call-done = bf16[256,2048]{1,0:T(8,128)(2,1)} async-done(((bf16[16,2048]{1,0:T(8,128)(2,1)}), bf16[256,2048]{1,0:T(8,128)(2,1)}) %all-gather.4.cloned.1.call-update) | async-done | bytes 1048592 | tf_op jit(solution)/shard_map/all_gather | solution.py:47
  51.4 2.3 %copy.58 = bf16[256,2048]{0,1:T(8,128)(2,1)} copy(bf16[256,2048]{1,0:T(8,128)(2,1)} %all-gather.4.cloned.1.call-done) | data formatting | bytes 2097152 | tf_op jit(solution)/shard_map/all_gather | solution.py:47
  53.6 1.8 bitcast_reduce_fusion
  56.1 34.3 %all-gather.6.cloned.1.call-done = bf16[256,2048]{1,0:T(8,128)(2,1)} async-done(((bf16[16,2048]{1,0:T(8,128)(2,1)}), bf16[256,2048]{1,0:T(8,128)(2,1)}) %all-gather.6.cloned.1.call-update) | async-done | bytes 1048592 | tf_op jit(solution)/shard_map/all_gather | solution.py:48
  90.4 2.3 copy.63
  92.7 2.2 fusion.3
  94.9 0.8 fusion.13
  96.5 3.1 %fusion.19 = f32[16,256,128]{1,2,0:T(8,128)} fusion(bf16[128,16,128]{0,2,1:T(8,128)(2,1)} %copy.80, f32[16,256,128]{2,1,0:T(8,128)S(1)} %get-tuple-element.26, f32[16,128]{1,0:T(8,128)S(1)} %get-tuple-element.16, pred[256]{0:T(512)(128)(4,1)S(1)} %fusion.48), kind=kOutput, calls=%fused_computation.31 | convolution fusion | flops 136314880 | bytes 4727040 | tf_op jit(solution)/shard_map/hsn,shd->nhd/dot_general | solution.py:78
  99.6 0.9 multiply_convert_fusion
  100.5 1.0 copy-done.10
  101.9 1.8 copy.79
  103.7 4.5 %pad_maximum_fusion = f32[256,4096]{0,1:T(8,128)} fusion(f32[256,2048]{0,1:T(8,128)} %bitcast.142, f32[256,2048]{0,1:T(8,128)} %bitcast.143), kind=kLoop, calls=%fused_computation | loop fusion | flops 1048576 | bytes 8388608 | tf_op jit(solution)/shard_map/concatenate | solution.py:80
  108.2 5.6 %copy.125 = f32[256,4096]{1,0:T(8,128)} copy(f32[256,4096]{0,1:T(8,128)} %pad_maximum_fusion) | data formatting | bytes 8388608
  113.8 1.2 copy-done.2
  115.0 1.6 fusion.17
  117.2 0.8 copy-done.9
  118.3 1.0 copy.87
  119.3 66.5 %reduce-scatter.4.cloned.1.call-done = f32[16,4096]{1,0:T(8,128)} async-done(((f32[256,4096]{1,0:T(8,128)}), f32[16,4096]{1,0:T(8,128)}) %reduce-scatter.4.cloned.1.call-update) | async-done | bytes 262160
  185.8 1.0 fusion.56
  187.8 1.3 multiply_reduce_fusion
  191.6 19.2 %all-gather = f32[128,16]{1,0:T(8,128)S(1)} all-gather(f32[8,16]{1,0:T(8,128)S(1)} %add_bitcast_fusion), channel_id=2, replica_groups=mesh['groups'=2,'ctx'=16] {'ctx'}, dimensions={0}, use_global_device_ids=true | all-gather | bytes 8704 | tf_op jit(solution)/shard_map/all_gather | solution.py:109
  211.5 2.4 %broadcast_multiply_fusion = (f32[16,16,128,8]{2,0,3,1:T(8,128)}, f32[16,16,128,8]{2,0,3,1:T(8,128)}) fusion(f32[16,16,128]{2,0,1:T(8,128)S(1)} %bitcast.155, f32[16,8]{0,1:T(8,128)} %bitcast.163, f32[16,16,128]{2,0,1:T(8,128)S(1)} %bitcast.156), kind=kLoop, calls=%fused_computation.55 | loop fusion | flops 524288 | bytes 2359808 | tf_op jit(solution)/shard_map/chd,sh->cshd/dot_general | solution.py:100
  213.9 1.6 copy.86
  215.5 1.3 fusion.18
  216.8 2.1 copy.89
  218.9 1.6 copy.82
  220.9 1.0 copy.88
  (73 shorter events, 10.1 us)
Async XLA Ops:
  7.2 5.2 %copy-start.4 = (bf16[128,2048]{1,0:T(8,128)(2,1)S(1)}, bf16[128,2048]{1,0:T(8,128)(2,1)}, u32[]{:S(2)}) copy-start(bf16[128,2048]{1,0:T(8,128)(2,1)} %param.6) | copy-start | bytes 1572868
  7.2 5.5 %copy-start.16 = (bf16[128,2048]{1,0:T(8,128)(2,1)S(1)}, bf16[128,2048]{1,0:T(8,128)(2,1)}, u32[]{:S(2)}) copy-start(bf16[128,2048]{1,0:T(8,128)(2,1)} %param.5) | copy-start | bytes 1572868
  7.2 44.2 %all-gather.4.cloned.1.call-start = ((), (), s32[]{:S(2)}) async-start(), calls=%async_computation.1 | async-start | bytes 1114112 | tf_op jit(solution)/shard_map/all_gather | solution.py:47
  8.1 4.8 %copy-start.17 = (bf16[128,2048]{1,0:T(8,128)(2,1)S(1)}, bf16[128,2048]{1,0:T(8,128)(2,1)}, u32[]{:S(2)}) copy-start(bf16[128,2048]{1,0:T(8,128)(2,1)} %param.8) | copy-start | bytes 1572868
  10.2 80.2 %all-gather.6.cloned.1.call-start = ((), (), s32[]{:S(2)}) async-start(), calls=%async_computation.2 | async-start | bytes 1114112 | tf_op jit(solution)/shard_map/all_gather | solution.py:48
  12.3 173.5 %reduce-scatter.4.cloned.1.call-start = ((), (), s32[]{:S(2)}) async-start(), calls=%async_computation.3 | async-start | bytes 4456448
  12.6 2.1 copy-start.8
  14.7 1.0 copy-start
  92.7 2.2 copy-start.1
  92.7 2.2 copy-start.14
  94.9 19.0 %copy-start.18 = (f32[16,128]{1,0:T(8,128)}, f32[16,128]{1,0:T(8,128)S(1)}, u32[]{:S(2)}) copy-start(f32[16,128]{1,0:T(8,128)S(1)} %get-tuple-element.16) | copy-start | bytes 24580
  96.5 3.1 %copy-start.6 = (bf16[128,16,128]{0,2,1:T(8,128)(2,1)S(1)}, bf16[128,16,128]{0,2,1:T(8,128)(2,1)}, u32[]{:S(2)}) copy-start(bf16[128,16,128]{0,2,1:T(8,128)(2,1)} %copy.80) | copy-start | bytes 1572868
  96.5 3.1 %copy-start.15 = (bf16[256,2048]{0,1:T(8,128)(2,1)S(1)}, bf16[256,2048]{0,1:T(8,128)(2,1)}, u32[]{:S(2)}) copy-start(bf16[256,2048]{0,1:T(8,128)(2,1)} %copy.63) | copy-start | bytes 3145732
  100.5 1.0 copy-start.10
  113.8 1.2 copy-start.2
  115.0 1.6 copy-start.3
  115.0 1.7 copy-start.11
  116.7 1.5 copy-start.12
  116.7 1.2 copy-start.9
  187.7 2.9 %copy-start.5 = (bf16[128,2048]{1,0:T(8,128)(2,1)S(1)}, bf16[128,2048]{1,0:T(8,128)(2,1)}, u32[]{:S(2)}) copy-start(bf16[128,2048]{1,0:T(8,128)(2,1)} %param.6) | copy-start | bytes 1572868
  211.5 4.0 %copy-start.7 = (bf16[128,16,128]{0,2,1:T(8,128)(2,1)S(1)}, bf16[128,16,128]{0,2,1:T(8,128)(2,1)}, u32[]{:S(2)}) copy-start(bf16[128,16,128]{0,2,1:T(8,128)(2,1)} %copy.80) | copy-start | bytes 1572868
  211.5 4.0 %copy-start.19 = (f32[16,128]{1,0:T(8,128)S(1)}, f32[16,128]{1,0:T(8,128)}, u32[]{:S(2)}) copy-start(f32[16,128]{1,0:T(8,128)} %copy-done.18) | copy-start | bytes 24580
  216.8 3.7 %copy-start.13 = (bf16[16,128,128]{1,2,0:T(8,128)(2,1)S(1)}, bf16[16,128,128]{1,2,0:T(8,128)(2,1)}, u32[]{:S(2)}) copy-start(bf16[16,128,128]{1,2,0:T(8,128)(2,1)} %copy-done.12) | copy-start | bytes 1572868
Sparse Core Ops, SparseCore 0:
  10.7 40.5 all-gather.3
  53.5 36.8 all-gather.5
  114.0 71.7 reduce-scatter.3
